TPU v7x, 128 devices: a whole 4x4x4 slice. The times are simulated.
128 devices in a mesh: pipe: 4 (over z), seq: 16 (over y, x), cfg: 2 (over core).
Axes of the slice: x: 4, y: 4, z: 4, core: 2. Of those that a mesh axis runs over, the one named last changes fastest.
Arguments:
- hidden: bfloat16 [2, 4, 2048, 5120], P('cfg', 'pipe', 'seq'), may hold values from -6 to 6
- qkv_weight: bfloat16 [4, 5120, 3, 4096], P('pipe', None, None, 'seq'), may hold values from -1 to 1
- out_weight: bfloat16 [4, 4096, 5120], P('pipe', 'seq'), may hold values from -0.09375 to 0.09375
- qk_gain: float32 [4, 2, 4096], P('pipe', None, 'seq'), may hold values from 0 to 8
- stale_kv: bfloat16 [2, 4, 2, 4096, 4096], P('cfg', 'pipe', None, None, 'seq'), may hold values from -6 to 6
- modulation: float32 [4, 50, 3, 5120], P('pipe'), may hold values from -3 to 3
- head_mod: float32 [50, 2, 5120], replicated, may hold values from -3 to 3
- head_weight: bfloat16 [5120, 64], replicated, may hold values from -0.078125 to 0.078125
- patch_index: int32 [1], replicated, may hold values from 0 to 1
- timestep: int32 [1], replicated, may hold values from 0 to 49
Outputs:
- forwarded: bfloat16 [2, 4, 2048, 5120], P('cfg', 'pipe', 'seq')
- fresh_kv: bfloat16 [2, 4, 2, 2048, 4096], P('cfg', 'pipe', None, None, 'seq')
- guided: float32 [4, 2048, 64], P('pipe', 'seq', 'cfg')
All inputs are finite; a program needn't handle non-finite values.
Results may differ from a plain program's by a relative error of at most 0.01.
Values may be sent and summed in bfloat16 or wider, within the bound.
No kernel may reach another device: no remote copies, remote signals or barrier semaphores. Data moves between devices by JAX's collectives and lax.ppermute only.
A program may use at most 128 MiB of HBM per device.

v0:
```python
import math
import jax
import jax.numpy as jnp
from jax import lax
from jax.sharding import PartitionSpec as P

HEAD = 128
NPATCH = 2
epsilon = 1e-06
guidance = 5.0


def passed_along(block, axis, distance):
    devices = range(lax.axis_size(axis))
    route = [((i - distance) % len(devices), i) for i in devices]
    return lax.ppermute(block, axis, route)


def partner_2(shard, axis, stride):
    return lax.ppermute(shard, axis, [(i, i ^ 1 << stride) for i in range(lax.axis_size(axis))])


def modulate(inputs, shift_row, scale_row):
    values = inputs.astype(jnp.float32)
    center = jnp.mean(values, axis=-1, keepdims=True)
    spread = jnp.mean(jnp.square(values - center), axis=-1, keepdims=True)
    return (values - center) * lax.rsqrt(spread + epsilon) * (1.0 + scale_row) + shift_row


def per_device(
    hidden,
    qkv_weight,
    out_weight,
    qk_gain,
    stale_kv,
    modulation,
    head_mod,
    head_weight,
    patch_index,
    timestep,
):
    tokens_in = hidden[0, 0]
    step_row = timestep[0]
    mod_rows = lax.dynamic_index_in_dim(modulation[0], step_row, 0, keepdims=False)
    head_rows = lax.dynamic_index_in_dim(head_mod, step_row, 0, keepdims=False)
    in_weight = qkv_weight[0]
    model_width = in_weight.shape[0]
    local_width = in_weight.shape[2]
    in_weight = in_weight.reshape(model_width, 3 * local_width)
    normed = modulate(tokens_in, mod_rows[0], mod_rows[1]).astype(jnp.bfloat16)
    projections = jnp.dot(
        lax.all_gather(normed, "seq", axis=0, tiled=True),
        in_weight,
        preferred_element_type=jnp.float32,
    )
    patch_tokens = projections.shape[0]
    queries = projections[:, :local_width]
    key_cols = projections[:, local_width : 2 * local_width]
    value_cols = projections[:, 2 * local_width :]
    square_sums = lax.psum(
        (jnp.sum(jnp.square(queries), axis=-1), jnp.sum(jnp.square(key_cols), axis=-1)), "seq"
    )
    full_width = local_width * lax.axis_size("seq")
    qk_gains = qk_gain[0]
    query_scale = lax.rsqrt(square_sums[0] / full_width + epsilon)[:, None]
    key_scale = lax.rsqrt(square_sums[1] / full_width + epsilon)[:, None]
    query_normed = (queries * query_scale * qk_gains[0]).astype(jnp.bfloat16)
    key_normed = (key_cols * key_scale * qk_gains[1]).astype(jnp.bfloat16)
    value_normed = value_cols.astype(jnp.bfloat16)
    section_index = lax.axis_index("pipe")
    patch_slot = jnp.mod(patch_index[0] - section_index, NPATCH)
    first_row = patch_slot * patch_tokens
    key_set = lax.dynamic_update_slice(stale_kv[0, 0, 0], key_normed, (first_row, jnp.int32(0)))
    value_set = lax.dynamic_update_slice(stale_kv[0, 0, 1], value_normed, (first_row, jnp.int32(0)))
    seq_rows = key_set.shape[0]
    heads_here = local_width // HEAD
    key_heads = key_set.reshape(seq_rows, heads_here, HEAD)
    value_heads = value_set.reshape(seq_rows, heads_here, HEAD)
    block_rows = math.gcd(patch_tokens, 512)
    block_count = patch_tokens // block_rows

    def attend(query_block):
        scores = jnp.einsum(
            "qhc,khc->hqk", query_block, key_heads, preferred_element_type=jnp.float32
        ) * HEAD ** (-0.5)
        top = jnp.max(scores, axis=-1, keepdims=True)
        expo = jnp.exp(scores - top)
        weights = (expo / jnp.sum(expo, axis=-1, keepdims=True)).astype(jnp.bfloat16)
        mixed = jnp.einsum("hqk,khc->qhc", weights, value_heads, preferred_element_type=jnp.float32)
        return mixed.astype(jnp.bfloat16).reshape(block_rows, local_width)

    attended = lax.map(attend, query_normed.reshape(block_count, block_rows, heads_here, HEAD))
    attended = attended.reshape(patch_tokens, local_width)
    out_rows = out_weight[0]
    projected = lax.psum_scatter(
        jnp.dot(attended, out_rows, preferred_element_type=jnp.float32).astype(jnp.bfloat16),
        "seq",
        scatter_dimension=0,
        tiled=True,
    ).astype(jnp.float32)
    block_out = (tokens_in.astype(jnp.float32) + mod_rows[2] * projected).astype(jnp.bfloat16)
    forwarded = passed_along(block_out, "pipe", 1)
    normed_out = modulate(block_out, head_rows[0], head_rows[1]).astype(jnp.bfloat16)
    readout = jnp.dot(normed_out, head_weight, preferred_element_type=jnp.float32)
    branch_index = lax.axis_index("cfg")
    half_width = readout.shape[1] // 2
    partner = partner_2(readout.astype(jnp.bfloat16), "cfg", 0).astype(readout.dtype)
    conditional = jnp.where(branch_index == 0, readout, partner)
    unconditional = jnp.where(branch_index == 0, partner, readout)
    combined = unconditional + guidance * (conditional - unconditional)
    guided = lax.dynamic_slice_in_dim(combined, branch_index * half_width, half_width, 1)
    fresh_pair = jnp.stack([key_normed, value_normed])
    return (forwarded[None, None], fresh_pair[None, None], guided[None])


def solution(mesh):
    return jax.shard_map(
        per_device,
        mesh=mesh,
        in_specs=(
            P("cfg", "pipe", "seq", None),
            P("pipe", None, None, "seq"),
            P("pipe", "seq", None),
            P("pipe", None, "seq"),
            P("cfg", "pipe", None, None, "seq"),
            P("pipe", None, None, None),
            P(),
            P(),
            P(),
            P(),
        ),
        out_specs=(
            P("cfg", "pipe", "seq", None),
            P("cfg", "pipe", None, None, "seq"),
            P("pipe", "seq", "cfg"),
        ),
        check_vma=False,
    )
```

profile of v0, /device:TPU:0, one launch (start us, length us, event | category | flops | bytes accessed | tf_op | source)
XLA Modules:
  0.0 539.0 jit_solution(13400286598347990033)
XLA Ops:
  7.2 0.0 copy-start
  7.2 0.0 all-gather.2.cloned.1.call-start
  8.0 1.6 convert_reduce_fusion.1
  9.6 1.8 fusion.35
  11.4 1.4 constant_dynamic-slice_fusion
  12.8 2.9 fusion.38
  15.8 0.0 all-gather.2.cloned.1.call-update
  15.8 0.0 reduce-scatter.2.cloned.1.call-start
  16.5 10.7 %copy.18 = bf16[1,5120,3,256]{1,3,2,0:T(8,128)(2,1)} copy(bf16[1,5120,3,256]{3,1,2,0:T(8,128)(2,1)} %param.13) | data formatting | bytes 15728640 | tf_op args[1]
  27.3 5.1 slice_bitcast_fusion
  32.4 0.0 copy-start.5
  32.4 4.1 copy.28
  36.5 0.0 copy-done.5
  36.5 114.6 %all-gather.2.cloned.1.call-done = bf16[2048,5120]{1,0:T(8,128)(2,1)} async-done(((bf16[128,5120]{1,0:T(8,128)(2,1)}), bf16[2048,5120]{1,0:T(8,128)(2,1)}) %all-gather.2.cloned.1.call-update) | async-done | bytes 20971536 | tf_op jit(solution)/shard_map/all_gather | solution.py:52
  151.0 20.4 %fusion.57 = f32[2048,768]{0,1:T(8,128)S(1)} fusion(bf16[2048,5120]{1,0:T(8,128)(2,1)} %all-gather.2.cloned.1.call-done, bf16[5120,768]{0,1:T(8,128)(2,1)} %bitcast.88), kind=kOutput, calls=%fused_computation.71 | convolution fusion | flops 16106127360 | bytes 35127296 | tf_op jit(solution)/shard_map/dot_general | solution.py:51
  171.4 0.0 copy-start.1
  171.4 2.7 copy-done.1
  174.1 0.4 multiply_reduce_fusion.1
  174.5 72.4 %all-reduce = (f32[2048]{0:T(1024)S(1)}, f32[2048]{0:T(1024)S(1)}) all-reduce(f32[2048]{0:T(1024)S(1)} %get-tuple-element.48, f32[2048]{0:T(1024)S(1)} %get-tuple-element.47), channel_id=1, replica_groups=mesh['pipe'=4,'seq'=16,'cfg'=2] {'seq'}, use_global_device_ids=true, to_apply=%region_3.4 | all-reduce | flops 4096 | bytes 32768 | tf_op jit(solution)/shard_map/psum | solution.py:60
  246.9 3.8 fusion.54
  250.7 2.3 copy.20
  253.0 2.3 constant_dynamic-update-slice_fusion.1
  255.2 4.1 copy.21
  259.3 4.1 copy.23
  263.4 4.0 fusion.47
  267.4 2.6 reshape.79
  270.0 2.6 copy.22
  272.7 82.0 %while.10 = (s32[]{:T(128)}, bf16[4,512,256]{2,1,0:T(8,128)(2,1)}, bf16[4,512,2,128]{3,1,2,0:T(8,128)(2,1)}, bf16[4096,2,128]{2,0,1:T(8,128)(2,1)}, bf16[4096,2,128]{0,2,1:T(8,128)(2,1)}, /*index=5*/s32[]{:T(128)}) while((s32[]{:T(128)}, bf16[4,512,256]{2,1,0:T(8,128)(2,1)}, bf16[4,512,2,128]{3,1,2,0:T(8,128)(2,1)}, ...), condition=%wide.region_9.10_spmd, body=%wide.region_6.9_spmd.sunk | while | flops 2168590336 | bytes 39330884 | solution.py:92
  272.7 10.3 %fusion.73 = (f32[2,512]{1,0:T(2,128)S(1)}, f32[2,512,4096]{2,1,0:T(8,128)}) fusion(bf16[4096,2,128]{2,0,1:T(8,128)(2,1)} %get-tuple-element.132, bf16[4,512,2,128]{3,1,2,0:T(8,128)(2,1)} %get-tuple-element.131, s32[]{:T(128)} %get-tuple-element.123), kind=kOutput, calls=%fused_computation.67.clone.1 | convolution fusion | flops 1086328832 | bytes 19141120 | tf_op jit(solution)/shard_map/while/body/eval_jaxpr/sub | solution.py:87
  282.9 9.3 %fusion.74 = bf16[2,512,128]{1,2,0:T(8,128)(2,1)S(1)} fusion(bf16[4096,2,128]{0,2,1:T(8,128)(2,1)} %get-tuple-element.133, f32[2,512,4096]{2,1,0:T(8,128)} %get-tuple-element.115, f32[2,512]{1,0:T(2,128)S(1)} %get-tuple-element.116), kind=kOutput, calls=%fused_computation.8.clone.1 | convolution fusion | flops 1082261504 | bytes 19140608 | tf_op jit(solution)/shard_map/while/body/eval_jaxpr/hqk,khc->qhc/dot_general | solution.py:89
  292.3 0.1 copy.30
  292.4 0.7 constant_dynamic-update-slice_fusion.4
  293.2 10.3 %fusion.73 = (f32[2,512]{1,0:T(2,128)S(1)}, f32[2,512,4096]{2,1,0:T(8,128)}) fusion(bf16[4096,2,128]{2,0,1:T(8,128)(2,1)} %get-tuple-element.132, bf16[4,512,2,128]{3,1,2,0:T(8,128)(2,1)} %get-tuple-element.131, s32[]{:T(128)} %get-tuple-element.123), kind=kOutput, calls=%fused_computation.67.clone.1 | convolution fusion | flops 1086328832 | bytes 19141120 | tf_op jit(solution)/shard_map/while/body/eval_jaxpr/sub | solution.py:87
  303.4 9.3 %fusion.74 = bf16[2,512,128]{1,2,0:T(8,128)(2,1)S(1)} fusion(bf16[4096,2,128]{0,2,1:T(8,128)(2,1)} %get-tuple-element.133, f32[2,512,4096]{2,1,0:T(8,128)} %get-tuple-element.115, f32[2,512]{1,0:T(2,128)S(1)} %get-tuple-element.116), kind=kOutput, calls=%fused_computation.8.clone.1 | convolution fusion | flops 1082261504 | bytes 19140608 | tf_op jit(solution)/shard_map/while/body/eval_jaxpr/hqk,khc->qhc/dot_general | solution.py:89
  312.8 0.1 copy.30
  312.9 0.7 constant_dynamic-update-slice_fusion.4
  313.7 10.3 %fusion.73 = (f32[2,512]{1,0:T(2,128)S(1)}, f32[2,512,4096]{2,1,0:T(8,128)}) fusion(bf16[4096,2,128]{2,0,1:T(8,128)(2,1)} %get-tuple-element.132, bf16[4,512,2,128]{3,1,2,0:T(8,128)(2,1)} %get-tuple-element.131, s32[]{:T(128)} %get-tuple-element.123), kind=kOutput, calls=%fused_computation.67.clone.1 | convolution fusion | flops 1086328832 | bytes 19141120 | tf_op jit(solution)/shard_map/while/body/eval_jaxpr/sub | solution.py:87
  323.9 9.3 %fusion.74 = bf16[2,512,128]{1,2,0:T(8,128)(2,1)S(1)} fusion(bf16[4096,2,128]{0,2,1:T(8,128)(2,1)} %get-tuple-element.133, f32[2,512,4096]{2,1,0:T(8,128)} %get-tuple-element.115, f32[2,512]{1,0:T(2,128)S(1)} %get-tuple-element.116), kind=kOutput, calls=%fused_computation.8.clone.1 | convolution fusion | flops 1082261504 | bytes 19140608 | tf_op jit(solution)/shard_map/while/body/eval_jaxpr/hqk,khc->qhc/dot_general | solution.py:89
  333.3 0.1 copy.30
  333.4 0.7 constant_dynamic-update-slice_fusion.4
  334.1 10.3 %fusion.73 = (f32[2,512]{1,0:T(2,128)S(1)}, f32[2,512,4096]{2,1,0:T(8,128)}) fusion(bf16[4096,2,128]{2,0,1:T(8,128)(2,1)} %get-tuple-element.132, bf16[4,512,2,128]{3,1,2,0:T(8,128)(2,1)} %get-tuple-element.131, s32[]{:T(128)} %get-tuple-element.123), kind=kOutput, calls=%fused_computation.67.clone.1 | convolution fusion | flops 1086328832 | bytes 19141120 | tf_op jit(solution)/shard_map/while/body/eval_jaxpr/sub | solution.py:87
  344.4 9.4 %fusion.74 = bf16[2,512,128]{1,2,0:T(8,128)(2,1)S(1)} fusion(bf16[4096,2,128]{0,2,1:T(8,128)(2,1)} %get-tuple-element.133, f32[2,512,4096]{2,1,0:T(8,128)} %get-tuple-element.115, f32[2,512]{1,0:T(2,128)S(1)} %get-tuple-element.116), kind=kOutput, calls=%fused_computation.8.clone.1 | convolution fusion | flops 1082261504 | bytes 19140608 | tf_op jit(solution)/shard_map/while/body/eval_jaxpr/hqk,khc->qhc/dot_general | solution.py:89
  353.8 0.1 copy.30
  353.9 0.7 constant_dynamic-update-slice_fusion.4
  354.6 0.0 copy-done
  354.6 11.2 %convolution_convert_fusion = bf16[2048,5120]{1,0:T(8,128)(2,1)} fusion(bf16[2048,256]{1,0:T(8,128)(2,1)} %bitcast.91, bf16[1,256,5120]{2,1,0:T(8,128)(2,1)S(1)} %copy-done), kind=kOutput, calls=%fused_computation.18 | convolution fusion | flops 5379194880 | bytes 24641536 | tf_op jit(solution)/shard_map/dot_general | solution.py:96
  365.9 0.0 reduce-scatter.2.cloned.1.call-update
  365.9 0.9 dynamic-slice_add_fusion
  366.8 127.4 %reduce-scatter.2.cloned.1.call-done = bf16[128,5120]{1,0:T(8,128)(2,1)} async-done(((bf16[2048,5120]{1,0:T(8,128)(2,1)}), bf16[128,5120]{1,0:T(8,128)(2,1)}) %reduce-scatter.2.cloned.1.call-update) | async-done | bytes 1310736 | tf_op jit(solution)/shard_map/reduce_scatter | solution.py:95
  494.2 0.0 copy-done.4
  494.2 3.3 convert_reduce_fusion
  497.5 1.6 collective-permute-start
  499.1 2.0 fusion.31
  501.1 0.0 copy-done.6
  501.1 2.1 fusion.56
  503.2 0.1 collective-permute-start.1
  503.3 0.0 copy-done.2
  503.3 0.0 copy-done.3
  503.3 1.5 maximum_bitcast_fusion
  504.8 3.9 copy.25
  508.8 0.0 collective-permute-done.1
  508.8 0.6 fusion.46
  509.4 20.3 %collective-permute-done = bf16[128,5120]{1,0:T(8,128)(2,1)} collective-permute-done((bf16[128,5120]{1,0:T(8,128)(2,1)}, bf16[128,5120]{1,0:T(8,128)(2,1)}, u32[]{:S(2)}, u32[]{:S(2)}) %collective-permute-start) | collective-permute-done | bytes 1310752 | tf_op jit(solution)/shard_map/ppermute | solution.py:16
  529.7 2.5 copy.43
  (11 shorter events, 0.0 us)
Async XLA Ops:
  7.2 347.5 %copy-start = (bf16[1,256,5120]{2,1,0:T(8,128)(2,1)S(1)}, bf16[1,256,5120]{2,1,0:T(8,128)(2,1)}, u32[]{:S(2)}) copy-start(bf16[1,256,5120]{2,1,0:T(8,128)(2,1)} %param.14) | copy-start | bytes 7864324
  7.2 143.8 %all-gather.2.cloned.1.call-start = ((), (), s32[]{:S(2)}) async-start(), calls=%async_computation.1 | async-start | bytes 22282240 | tf_op jit(solution)/shard_map/all_gather | solution.py:52
  15.8 478.4 %reduce-scatter.2.cloned.1.call-start = ((), (), s32[]{:S(2)}) async-start(), calls=%async_computation.2 | async-start | bytes 22282240 | tf_op jit(solution)/shard_map/reduce_scatter | solution.py:95
  32.4 4.1 copy-start.5
  171.4 2.7 copy-start.1
  365.9 128.4 %copy-start.4 = (f32[1,1,1,5120]{3,0,2,1:T(1,128)S(1)}, f32[1,1,1,5120]{3,0,2,1:T(1,128)}, u32[]{:S(2)}) copy-start(f32[1,1,1,5120]{3,0,2,1:T(1,128)} %get-tuple-element.71) | copy-start | bytes 61444
  494.2 6.8 %copy-start.6 = (bf16[5120,64]{0,1:T(8,128)(2,1)S(1)}, bf16[5120,64]{0,1:T(8,128)(2,1)}, u32[]{:S(2)}) copy-start(bf16[5120,64]{0,1:T(8,128)(2,1)} %param.19) | copy-start | bytes 1966084
  497.5 32.1 %collective-permute-start = (bf16[128,5120]{1,0:T(8,128)(2,1)}, bf16[128,5120]{1,0:T(8,128)(2,1)}, u32[]{:S(2)}, u32[]{:S(2)}) collective-permute-start(bf16[128,5120]{1,0:T(8,128)(2,1)} %get-tuple-element.62), channel_id=1, source_target_pairs={{96,0},{0,32},{32,64},{64,96},{97,1},{1,33},{33,65},{65,97},{98,2}... | collective-permute-start | bytes 3932168 | tf_op jit(solution)/shard_map/ppermute | solution.py:16
  499.1 4.2 copy-start.2
  499.1 4.2 copy-start.3
  503.2 5.6 %collective-permute-start.1 = (bf16[128,64]{0,1:T(8,128)(2,1)S(1)}, bf16[128,64]{0,1:T(8,128)(2,1)S(1)}, u32[]{:S(2)}, u32[]{:S(2)}) collective-permute-start(bf16[128,64]{0,1:T(8,128)(2,1)S(1)} %get-tuple-element.78), channel_id=1, source_target_pairs={{0,1},{1,0},{2,3},{3,2},{4,5},{5,4},{6,7},{7,6},{8,9},{9,8},{10,11... | collective-permute-start | bytes 49160 | tf_op jit(solution)/shard_map/ppermute | solution.py:20
Sparse Core Ops, SparseCore 0:
  15.9 135.0 all-gather.1
  366.0 128.1 reduce-scatter.1
where the time goes:
time: 540 us; the launch traced here: 539 us
  waiting for transfers between devices  262 us (49%)
  matrix products  112 us (21%)
  blocking collectives  72.4 us (13%)
  local copies, waits for them, and re-layouts  50.4 us (9%)
  other arithmetic  24.3 us (4%)
  between operations  15.6 us (3%)
    reduce_scatter x1, waiting for transfers between devices, per_device(): lax.psum_scatter(jnp.dot(attended, out_rows, preferred_element_type=jnp.f...  127 us
    all_gather x1, waiting for transfers between devices, per_device(): lax.all_gather(normed, 'seq', axis=0, tiled=True)  115 us
    psum x1, blocking collectives, per_device(): lax.psum((jnp.sum(jnp.square(queries), axis=-1), jnp.sum(jnp.square(key_c...  72.4 us
    sub x4, matrix products, attend(): expo = jnp.exp(scores - top)  41.1 us
    dot_general x4, matrix products, attend(): jnp.einsum('hqk,khc->qhc', weights, value_heads, preferred_element_type=j...  37.4 us
    unnamed x18, local copies, waits for them, and re-layouts  23.9 us
    dot_general x1, matrix products, per_device(): jnp.dot(lax.all_gather(normed, 'seq', axis=0, tiled=True), in_weight, pre...  20.4 us
    ppermute x1, waiting for transfers between devices, passed_along(): return lax.ppermute(block, axis, route)  20.3 us
  transfers between devices with their start and end apart: 4, of which 3 were waited for; matrix products, arithmetic and copies ran while one was open for 6% of the time, Pallas kernels for 0%

commit v1 on v0

--- a/solution.py
+++ b/solution.py
@@ -49,7 +49,15 @@
     in_weight = in_weight.reshape(model_width, 3 * local_width)
     normed = modulate(tokens_in, mod_rows[0], mod_rows[1]).astype(jnp.bfloat16)
     projections = jnp.dot(
-        lax.all_gather(normed, "seq", axis=0, tiled=True),
+        jnp.concatenate(
+            lax.all_to_all(
+                jnp.stack(lax.axis_size("seq") * [normed]),
+                axis_name="seq",
+                split_axis=0,
+                concat_axis=0,
+            ),
+            axis=0,
+        ),
         in_weight,
         preferred_element_type=jnp.float32,
     )

time: 540 us -> 730 us (1.35)
  waiting for transfers between devices: 262 us -> 441 us
    all_to_all x0 -> x1, waiting for transfers between devices: none -> 293 us  [per_device(): lax.all_to_all(jnp.stack(lax.axis_size('seq') * [normed]), axis_name='seq...]
    all_gather x1 -> x0, waiting for transfers between devices: 115 us -> none  [per_device(): lax.all_gather(normed, 'seq', axis=0, tiled=True)]
    another operation x0 -> x1, local copies, waits for them, and re-layouts: none -> 7.41 us  [per_device(): jnp.stack(lax.axis_size('seq') * [normed])]
  transfers between devices with their start and end apart: 4 -> 4, of which waited for: 3 -> 3; matrix products, arithmetic and copies ran while one was open for 6% -> 4% of each run, Pallas kernels for 0% -> 0%
where the time goes in v1:
time: 730 us; the launch traced here: 728 us
  waiting for transfers between devices  441 us (60%)
  matrix products  112 us (15%)
  blocking collectives  70.1 us (10%)
  local copies, waits for them, and re-layouts  57.2 us (8%)
  other arithmetic  23.2 us (3%)
  between operations  15.6 us (2%)
  starting transfers between devices  8.86 us (1%)
    all_to_all x1, waiting for transfers between devices, per_device(): lax.all_to_all(jnp.stack(lax.axis_size('seq') * [normed]), axis_name='seq...  293 us
    reduce_scatter x1, waiting for transfers between devices, per_device(): lax.psum_scatter(jnp.dot(attended, out_rows, preferred_element_type=jnp.f...  128 us
    psum x1, blocking collectives, per_device(): lax.psum((jnp.sum(jnp.square(queries), axis=-1), jnp.sum(jnp.square(key_c...  70.1 us
    sub x4, matrix products, attend(): expo = jnp.exp(scores - top)  41.1 us
    dot_general x4, matrix products, attend(): jnp.einsum('hqk,khc->qhc', weights, value_heads, preferred_element_type=j...  37.4 us
    unnamed x18, local copies, waits for them, and re-layouts  23.9 us
    dot_general x1, matrix products, per_device(): jnp.dot(jnp.concatenate(lax.all_to_all(jnp.stack(lax.axis_size('seq') * [...  20.4 us
    ppermute x1, waiting for transfers between devices, passed_along(): return lax.ppermute(block, axis, route)  20.3 us
  transfers between devices with their start and end apart: 4, of which 3 were waited for; matrix products, arithmetic and copies ran while one was open for 4% of the time, Pallas kernels for 0%

profile of v1, /device:TPU:0, one launch (start us, length us, event | category | flops | bytes accessed | tf_op | source)
XLA Modules:
  0.0 728.5 jit_solution(8972580006647074403)
XLA Ops:
  7.2 0.0 copy-start
  8.0 1.6 convert_reduce_fusion.1
  9.6 1.8 fusion.35
  11.4 1.4 constant_dynamic-slice_fusion
  12.8 1.9 fusion.38
  14.7 7.4 %stack.8 = bf16[16,128,5120]{2,1,0:T(8,128)(2,1)} broadcast(bf16[128,5120]{1,0:T(8,128)(2,1)S(1)} %fusion.38), dimensions={1,2} | broadcast | bytes 22282240 | tf_op jit(solution)/shard_map/stack | solution.py:54
  22.1 7.2 all-to-all-start
  29.3 0.0 reduce-scatter.2.cloned.1.call-start
  30.0 10.7 %copy.18 = bf16[1,5120,3,256]{1,3,2,0:T(8,128)(2,1)} copy(bf16[1,5120,3,256]{3,1,2,0:T(8,128)(2,1)} %param.13) | data formatting | bytes 15728640 | tf_op args[1]
  40.7 4.5 slice_bitcast_fusion
  45.2 0.0 copy-start.5
  45.2 4.1 copy.28
  49.3 0.0 copy-done.5
  49.3 292.7 %all-to-all-done = bf16[16,128,5120]{2,1,0:T(8,128)(2,1)} async-done(((bf16[16,128,5120]{2,1,0:T(8,128)(2,1)}), bf16[16,128,5120]{2,1,0:T(8,128)(2,1)}, u32[]{:S(2)}, u32[]{:S(2)}) %all-to-all-start) | async-done | bytes 20971552 | tf_op jit(solution)/shard_map/all_to_all | solution.py:53
  342.0 20.4 %fusion.57 = f32[2048,768]{0,1:T(8,128)S(1)} fusion(bf16[2048,5120]{1,0:T(8,128)(2,1)} %bitcast.8, bf16[5120,768]{0,1:T(8,128)(2,1)} %bitcast.89), kind=kOutput, calls=%fused_computation.71 | convolution fusion | flops 16106127360 | bytes 35127296 | tf_op jit(solution)/shard_map/dot_general | solution.py:51
  362.4 0.0 copy-start.1
  362.4 2.7 copy-done.1
  365.0 0.4 multiply_reduce_fusion.1
  365.4 70.1 %all-reduce = (f32[2048]{0:T(1024)S(1)}, f32[2048]{0:T(1024)S(1)}) all-reduce(f32[2048]{0:T(1024)S(1)} %get-tuple-element.48, f32[2048]{0:T(1024)S(1)} %get-tuple-element.47), channel_id=1, replica_groups=mesh['pipe'=4,'seq'=16,'cfg'=2] {'seq'}, use_global_device_ids=true, to_apply=%region_3.4 | all-reduce | flops 4096 | bytes 32768 | tf_op jit(solution)/shard_map/psum | solution.py:68
  435.5 3.8 fusion.54
  439.3 2.3 copy.20
  441.6 2.3 constant_dynamic-update-slice_fusion.1
  443.9 4.1 copy.21
  448.0 4.1 copy.23
  452.0 4.0 fusion.47
  456.0 2.6 reshape.119
  458.6 2.6 copy.22
  461.3 82.0 %while.10 = (s32[]{:T(128)}, bf16[4,512,256]{2,1,0:T(8,128)(2,1)}, bf16[4,512,2,128]{3,1,2,0:T(8,128)(2,1)}, bf16[4096,2,128]{2,0,1:T(8,128)(2,1)}, bf16[4096,2,128]{0,2,1:T(8,128)(2,1)}, /*index=5*/s32[]{:T(128)}) while((s32[]{:T(128)}, bf16[4,512,256]{2,1,0:T(8,128)(2,1)}, bf16[4,512,2,128]{3,1,2,0:T(8,128)(2,1)}, ...), condition=%wide.region_9.10_spmd, body=%wide.region_6.9_spmd.sunk | while | flops 2168590336 | bytes 39330884 | solution.py:100
  461.3 10.3 %fusion.73 = (f32[2,512]{1,0:T(2,128)S(1)}, f32[2,512,4096]{2,1,0:T(8,128)}) fusion(bf16[4096,2,128]{2,0,1:T(8,128)(2,1)} %get-tuple-element.132, bf16[4,512,2,128]{3,1,2,0:T(8,128)(2,1)} %get-tuple-element.131, s32[]{:T(128)} %get-tuple-element.123), kind=kOutput, calls=%fused_computation.67.clone.1 | convolution fusion | flops 1086328832 | bytes 19141120 | tf_op jit(solution)/shard_map/while/body/eval_jaxpr/sub | solution.py:95
  471.6 9.3 %fusion.74 = bf16[2,512,128]{1,2,0:T(8,128)(2,1)S(1)} fusion(bf16[4096,2,128]{0,2,1:T(8,128)(2,1)} %get-tuple-element.133, f32[2,512,4096]{2,1,0:T(8,128)} %get-tuple-element.115, f32[2,512]{1,0:T(2,128)S(1)} %get-tuple-element.116), kind=kOutput, calls=%fused_computation.8.clone.1 | convolution fusion | flops 1082261504 | bytes 19140608 | tf_op jit(solution)/shard_map/while/body/eval_jaxpr/hqk,khc->qhc/dot_general | solution.py:97
  480.9 0.1 copy.30
  481.1 0.7 constant_dynamic-update-slice_fusion.4
  481.8 10.3 %fusion.73 = (f32[2,512]{1,0:T(2,128)S(1)}, f32[2,512,4096]{2,1,0:T(8,128)}) fusion(bf16[4096,2,128]{2,0,1:T(8,128)(2,1)} %get-tuple-element.132, bf16[4,512,2,128]{3,1,2,0:T(8,128)(2,1)} %get-tuple-element.131, s32[]{:T(128)} %get-tuple-element.123), kind=kOutput, calls=%fused_computation.67.clone.1 | convolution fusion | flops 1086328832 | bytes 19141120 | tf_op jit(solution)/shard_map/while/body/eval_jaxpr/sub | solution.py:95
  492.0 9.4 %fusion.74 = bf16[2,512,128]{1,2,0:T(8,128)(2,1)S(1)} fusion(bf16[4096,2,128]{0,2,1:T(8,128)(2,1)} %get-tuple-element.133, f32[2,512,4096]{2,1,0:T(8,128)} %get-tuple-element.115, f32[2,512]{1,0:T(2,128)S(1)} %get-tuple-element.116), kind=kOutput, calls=%fused_computation.8.clone.1 | convolution fusion | flops 1082261504 | bytes 19140608 | tf_op jit(solution)/shard_map/while/body/eval_jaxpr/hqk,khc->qhc/dot_general | solution.py:97
  501.4 0.1 copy.30
  501.5 0.7 constant_dynamic-update-slice_fusion.4
  502.3 10.3 %fusion.73 = (f32[2,512]{1,0:T(2,128)S(1)}, f32[2,512,4096]{2,1,0:T(8,128)}) fusion(bf16[4096,2,128]{2,0,1:T(8,128)(2,1)} %get-tuple-element.132, bf16[4,512,2,128]{3,1,2,0:T(8,128)(2,1)} %get-tuple-element.131, s32[]{:T(128)} %get-tuple-element.123), kind=kOutput, calls=%fused_computation.67.clone.1 | convolution fusion | flops 1086328832 | bytes 19141120 | tf_op jit(solution)/shard_map/while/body/eval_jaxpr/sub | solution.py:95
  512.5 9.3 %fusion.74 = bf16[2,512,128]{1,2,0:T(8,128)(2,1)S(1)} fusion(bf16[4096,2,128]{0,2,1:T(8,128)(2,1)} %get-tuple-element.133, f32[2,512,4096]{2,1,0:T(8,128)} %get-tuple-element.115, f32[2,512]{1,0:T(2,128)S(1)} %get-tuple-element.116), kind=kOutput, calls=%fused_computation.8.clone.1 | convolution fusion | flops 1082261504 | bytes 19140608 | tf_op jit(solution)/shard_map/while/body/eval_jaxpr/hqk,khc->qhc/dot_general | solution.py:97
  521.9 0.1 copy.30
  522.0 0.7 constant_dynamic-update-slice_fusion.4
  522.8 10.3 %fusion.73 = (f32[2,512]{1,0:T(2,128)S(1)}, f32[2,512,4096]{2,1,0:T(8,128)}) fusion(bf16[4096,2,128]{2,0,1:T(8,128)(2,1)} %get-tuple-element.132, bf16[4,512,2,128]{3,1,2,0:T(8,128)(2,1)} %get-tuple-element.131, s32[]{:T(128)} %get-tuple-element.123), kind=kOutput, calls=%fused_computation.67.clone.1 | convolution fusion | flops 1086328832 | bytes 19141120 | tf_op jit(solution)/shard_map/while/body/eval_jaxpr/sub | solution.py:95
  533.0 9.4 %fusion.74 = bf16[2,512,128]{1,2,0:T(8,128)(2,1)S(1)} fusion(bf16[4096,2,128]{0,2,1:T(8,128)(2,1)} %get-tuple-element.133, f32[2,512,4096]{2,1,0:T(8,128)} %get-tuple-element.115, f32[2,512]{1,0:T(2,128)S(1)} %get-tuple-element.116), kind=kOutput, calls=%fused_computation.8.clone.1 | convolution fusion | flops 1082261504 | bytes 19140608 | tf_op jit(solution)/shard_map/while/body/eval_jaxpr/hqk,khc->qhc/dot_general | solution.py:97
  542.4 0.1 copy.30
  542.5 0.7 constant_dynamic-update-slice_fusion.4
  543.3 0.0 copy-done
  543.3 11.2 %convolution_convert_fusion = bf16[2048,5120]{1,0:T(8,128)(2,1)} fusion(bf16[2048,256]{1,0:T(8,128)(2,1)} %bitcast.92, bf16[1,256,5120]{2,1,0:T(8,128)(2,1)S(1)} %copy-done), kind=kOutput, calls=%fused_computation.18 | convolution fusion | flops 5379194880 | bytes 24641536 | tf_op jit(solution)/shard_map/dot_general | solution.py:104
  554.5 0.0 reduce-scatter.2.cloned.1.call-update
  554.5 0.9 dynamic-slice_add_fusion
  555.4 128.3 %reduce-scatter.2.cloned.1.call-done = bf16[128,5120]{1,0:T(8,128)(2,1)} async-done(((bf16[2048,5120]{1,0:T(8,128)(2,1)}), bf16[128,5120]{1,0:T(8,128)(2,1)}) %reduce-scatter.2.cloned.1.call-update) | async-done | bytes 1310736 | tf_op jit(solution)/shard_map/reduce_scatter | solution.py:103
  683.8 0.0 copy-done.4
  683.8 3.3 convert_reduce_fusion
  687.1 1.6 collective-permute-start
  688.6 2.0 fusion.31
  690.6 0.0 copy-done.6
  690.6 2.1 fusion.56
  692.7 0.1 collective-permute-start.1
  692.8 0.0 copy-done.2
  692.8 0.0 copy-done.3
  692.8 1.5 maximum_bitcast_fusion
  694.4 3.9 copy.25
  698.3 0.0 collective-permute-done.1
  698.3 0.6 fusion.46
  698.9 20.3 %collective-permute-done = bf16[128,5120]{1,0:T(8,128)(2,1)} collective-permute-done((bf16[128,5120]{1,0:T(8,128)(2,1)}, bf16[128,5120]{1,0:T(8,128)(2,1)}, u32[]{:S(2)}, u32[]{:S(2)}) %collective-permute-start) | collective-permute-done | bytes 1310752 | tf_op jit(solution)/shard_map/ppermute | solution.py:16
  719.2 2.5 copy.43
  (11 shorter events, 0.0 us)
Async XLA Ops:
  7.2 536.1 %copy-start = (bf16[1,256,5120]{2,1,0:T(8,128)(2,1)S(1)}, bf16[1,256,5120]{2,1,0:T(8,128)(2,1)}, u32[]{:S(2)}) copy-start(bf16[1,256,5120]{2,1,0:T(8,128)(2,1)} %param.14) | copy-start | bytes 7864324
  22.1 319.9 %all-to-all-start = ((bf16[16,128,5120]{2,1,0:T(8,128)(2,1)}), bf16[16,128,5120]{2,1,0:T(8,128)(2,1)}, u32[]{:S(2)}, u32[]{:S(2)}) async-start(bf16[16,128,5120]{2,1,0:T(8,128)(2,1)} %stack.8), calls=%async_computation | async-start | bytes 41943040 | tf_op jit(solution)/shard_map/all_to_all | solution.py:53
  29.3 654.5 %reduce-scatter.2.cloned.1.call-start = ((), (), s32[]{:S(2)}) async-start(), calls=%async_computation.2 | async-start | bytes 22282240 | tf_op jit(solution)/shard_map/reduce_scatter | solution.py:103
  45.2 4.1 copy-start.5
  362.4 2.7 copy-start.1
  554.5 129.2 %copy-start.4 = (f32[1,1,1,5120]{3,0,2,1:T(1,128)S(1)}, f32[1,1,1,5120]{3,0,2,1:T(1,128)}, u32[]{:S(2)}) copy-start(f32[1,1,1,5120]{3,0,2,1:T(1,128)} %get-tuple-element.71) | copy-start | bytes 61444
  683.8 6.9 copy-start.6
  687.1 32.1 %collective-permute-start = (bf16[128,5120]{1,0:T(8,128)(2,1)}, bf16[128,5120]{1,0:T(8,128)(2,1)}, u32[]{:S(2)}, u32[]{:S(2)}) collective-permute-start(bf16[128,5120]{1,0:T(8,128)(2,1)} %get-tuple-element.62), channel_id=1, source_target_pairs={{96,0},{0,32},{32,64},{64,96},{97,1},{1,33},{33,65},{65,97},{98,2}... | collective-permute-start | bytes 3932168 | tf_op jit(solution)/shard_map/ppermute | solution.py:16
  688.6 4.2 copy-start.2
  688.6 4.2 copy-start.3
  692.7 5.6 collective-permute-start.1
Sparse Core Ops, SparseCore 0:
  554.7 129.0 reduce-scatter.1
